TPU v7x, 512 devices: a whole 4x4x16 slice. The times are simulated.
512 devices in a mesh: replica: 64 (over z_hi, y, x, core), tensor: 8 (over z_lo).
Axes of the slice: x: 4, y: 4, z: 16 (z_hi: 2, z_lo: 8; z = z_hi * 8 + z_lo), core: 2. Of those that a mesh axis runs over, the one named last changes fastest.
Arguments:
- tokens: bfloat16 [32768, 8192], P(('replica', 'tensor')), may hold values from -6 to 6
- norm_gain: bfloat16 [8192], replicated, may hold values from 0.099609375 to 1.8984375
- key_weight: bfloat16 [64, 8192, 1024], P('replica', None, 'tensor'), may hold values from -0.0625 to 0.0625
- inner_params: bfloat16 [64, 8, 1024, 512], P('replica', 'tensor'), may hold values from -16 to 16
- outer_params: float32 [8, 1024, 512], P('tensor', 'replica'), may hold values from -6 to 6
- outer_momentum: float32 [8, 1024, 512], P('tensor', 'replica'), may hold values from -3 to 3
Outputs:
- key_rows: bfloat16 [32768, 1024], P('replica', 'tensor')
- new_outer: float32 [8, 1024, 512], P('tensor', 'replica')
- new_momentum: float32 [8, 1024, 512], P('tensor', 'replica')
- synced_params: bfloat16 [8, 1024, 512], P('tensor')
All inputs are finite; a program needn't handle non-finite values.
Results may differ from a plain program's by a relative error of at most 0.0049.
Values may be sent and summed in bfloat16 or wider, within the bound.
No kernel may reach another device: no remote copies, remote signals or barrier semaphores. Data moves between devices by JAX's collectives and lax.ppermute only.
A program may use at most 64 MiB of HBM per device.

v0:
```python
import math
import jax
import jax.numpy as jnp
from jax import lax
from jax.sharding import PartitionSpec as P

HD = 128
EPSILON = 1e-05
ROPE_BASE = 500000.0
LR_OUTER = 0.7
MOMENTUM_OUTER = 0.9


def rotate(keys_f32, positions):
    rows = keys_f32.shape[0]
    cols = keys_f32.shape[1]
    half = HD // 2
    shaped = keys_f32.reshape(rows, cols // HD, HD)
    index = jnp.arange(half).astype(jnp.float32)
    inverse = jnp.exp(-(2.0 * index / HD) * math.log(ROPE_BASE))
    angles = positions[:, None] * inverse[None, :]
    cosine = jnp.cos(angles)[:, None, :]
    sine = jnp.sin(angles)[:, None, :]
    first = shaped[:, :, :half]
    second = shaped[:, :, half:]
    joined = jnp.concatenate(
        [first * cosine - second * sine, second * cosine + first * sine], axis=-1
    )
    return joined.reshape(rows, cols)


def forward_keys(tokens, norm_gain, key_weight):
    block_f32 = tokens.astype(jnp.float32)
    scale = lax.rsqrt(jnp.mean(block_f32 * block_f32, axis=-1, keepdims=True) + EPSILON)
    normed = (block_f32 * scale * norm_gain.astype(jnp.float32)).astype(jnp.bfloat16)
    weight = key_weight[0]
    piece = lax.all_gather(normed, "tensor", axis=0, tiled=True)
    projected = jnp.dot(piece, weight, preferred_element_type=jnp.float32)
    positions = jnp.arange(piece.shape[0], dtype=jnp.int32).astype(jnp.float32)
    return rotate(projected, positions).astype(jnp.bfloat16)


def nesterov(outer_rows, moment_rows, summed, replicas):
    delta = outer_rows - summed / replicas
    moment_next = MOMENTUM_OUTER * moment_rows + delta
    outer_next = outer_rows - LR_OUTER * (delta + MOMENTUM_OUTER * moment_next)
    return (outer_next, moment_next)


def owned_sum(local_params):
    return lax.psum_scatter(
        local_params.astype(jnp.float32), "replica", scatter_dimension=0, tiled=True
    )


def sync_fragment(inner_params, outer_params, outer_momentum):
    replicas = lax.axis_size("replica")
    local_params = inner_params[0, 0]
    summed = owned_sum(local_params)
    outer_next, moment_next = nesterov(outer_params[0], outer_momentum[0], summed, replicas)
    synced = lax.all_gather(outer_next.astype(jnp.bfloat16), "replica", axis=0, tiled=True)
    return (outer_next[None], moment_next[None], synced[None])


def body(tokens, norm_gain, key_weight, inner_params, outer_params, outer_momentum):
    key_rows = forward_keys(tokens, norm_gain, key_weight)
    new_outer, new_momentum, synced_params = sync_fragment(
        inner_params, outer_params, outer_momentum
    )
    return (key_rows, new_outer, new_momentum, synced_params)


def solution(mesh):
    in_specs = (
        P(("replica", "tensor"), None),
        P(),
        P("replica", None, "tensor"),
        P("replica", "tensor", None, None),
        P("tensor", "replica", None),
        P("tensor", "replica", None),
    )
    out_specs = (
        P("replica", "tensor"),
        P("tensor", "replica", None),
        P("tensor", "replica", None),
        P("tensor", None, None),
    )
    return jax.shard_map(body, mesh=mesh, in_specs=in_specs, out_specs=out_specs, check_vma=False)
```

profile of v0, /device:TPU:1, one launch (start us, length us, event | category | flops | bytes accessed | tf_op | source)
XLA Modules:
  0.0 875.6 jit_solution(4072510112862424039)
XLA Ops:
  7.2 0.0 copy-start
  7.2 0.0 copy-start.5
  7.2 0.0 copy-start.1
  7.2 0.0 reduce-scatter.2.cloned.1.call-start
  7.2 3.0 bitcast_convert_fusion
  10.2 0.0 copy-start.3
  10.2 0.0 copy-start.4
  10.2 0.0 reduce-scatter.2.cloned.1.call-update
  10.3 0.0 all-gather.5.cloned.1.call-start
  10.3 0.0 copy-done.5
  10.3 0.0 copy-done.1
  10.4 0.3 fusion
  10.7 565.8 %reduce-scatter.2.cloned.1.call-done = f32[16,512]{1,0:T(8,128)} async-done(((f32[1024,512]{1,0:T(8,128)}), f32[16,512]{1,0:T(8,128)}) %reduce-scatter.2.cloned.1.call-update) | async-done | bytes 32784 | tf_op jit(solution)/shard_map/reduce_scatter | solution.py:51
  576.5 0.0 copy-done.3
  576.5 0.0 copy-done.4
  576.5 1.4 fusion.17
  577.9 0.0 all-gather.5.cloned.1.call-update
  577.9 0.0 all-gather.3.cloned.1.call-start
  578.0 1.3 fusion.2
  579.2 0.0 all-gather.3.cloned.1.call-update
  579.3 108.2 %all-gather.5.cloned.1.call-done = bf16[1024,512]{1,0:T(8,128)(2,1)} async-done(((bf16[16,512]{1,0:T(8,128)(2,1)}), bf16[1024,512]{1,0:T(8,128)(2,1)}) %all-gather.5.cloned.1.call-update) | async-done | bytes 1048592 | tf_op jit(solution)/shard_map/all_gather | solution.py:61
  687.5 0.0 copy-start.2
  687.5 173.0 %all-gather.3.cloned.1.call-done = bf16[512,8192]{1,0:T(8,128)(2,1)} async-done(((bf16[64,8192]{1,0:T(8,128)(2,1)}), bf16[512,8192]{1,0:T(8,128)(2,1)}) %all-gather.3.cloned.1.call-update) | async-done | bytes 8388624 | tf_op jit(solution)/shard_map/all_gather | solution.py:37
  860.5 0.0 copy-done
  860.5 6.3 fusion.5
  866.8 0.6 fusion.13
  867.4 0.8 copy.10
  868.1 0.0 copy-done.2
  868.2 1.0 copy.12
  (5 shorter events, 0.0 us)
Async XLA Ops:
  7.2 853.4 %copy-start = (bf16[1,8192,128]{2,1,0:T(8,128)(2,1)S(1)}, bf16[1,8192,128]{2,1,0:T(8,128)(2,1)}, u32[]{:S(2)}) copy-start(bf16[1,8192,128]{2,1,0:T(8,128)(2,1)} %param.8) | copy-start | bytes 6291460
  7.2 3.1 copy-start.5
  7.2 3.2 copy-start.1
  7.2 569.3 %reduce-scatter.2.cloned.1.call-start = ((), (), s32[]{:S(2)}) async-start(), calls=%async_computation.2 | async-start | bytes 2129920 | tf_op jit(solution)/shard_map/reduce_scatter | solution.py:51
  10.2 566.2 %copy-start.3 = (f32[1,16,512]{2,1,0:T(8,128)S(1)}, f32[1,16,512]{2,1,0:T(8,128)}, u32[]{:S(2)}) copy-start(f32[1,16,512]{2,1,0:T(8,128)} %param.11) | copy-start | bytes 98308
  10.2 566.2 %copy-start.4 = (f32[1,16,512]{2,1,0:T(8,128)S(1)}, f32[1,16,512]{2,1,0:T(8,128)}, u32[]{:S(2)}) copy-start(f32[1,16,512]{2,1,0:T(8,128)} %param.10) | copy-start | bytes 98308
  10.3 677.2 %all-gather.5.cloned.1.call-start = ((), (), s32[]{:S(2)}) async-start(), calls=%async_computation.3 | async-start | bytes 1064960 | tf_op jit(solution)/shard_map/all_gather | solution.py:61
  577.9 282.6 %all-gather.3.cloned.1.call-start = ((), (), s32[]{:S(2)}) async-start(), calls=%async_computation.1 | async-start | bytes 9437184 | tf_op jit(solution)/shard_map/all_gather | solution.py:37
  687.5 180.6 %copy-start.2 = (bf16[1024,512]{1,0:T(8,128)(2,1)S(1)}, bf16[1024,512]{1,0:T(8,128)(2,1)}, u32[]{:S(2)}) copy-start(bf16[1024,512]{1,0:T(8,128)(2,1)} %all-gather.5.cloned.1.call-done) | copy-start | bytes 3145732
Sparse Core Ops, SparseCore 0:
  10.8 565.6 reduce-scatter.1
  582.3 105.1 all-gather.4
  690.4 170.1 all-gather.2
where the time goes:
time: 876 us
  waiting for transfers between devices  847 us (97%)
  between operations  13.8 us (2%)
    reduce_scatter x1, waiting for transfers between devices, owned_sum(): lax.psum_scatter(local_params.astype(jnp.float32), 'replica', scatter_dim...  566 us
    all_gather x1, waiting for transfers between devices, forward_keys(): piece = lax.all_gather(normed, 'tensor', axis=0, tiled=True)  173 us
    all_gather x1, waiting for transfers between devices, sync_fragment(): lax.all_gather(outer_next.astype(jnp.bfloat16), 'replica', axis=0, tiled=...  108 us
  transfers between devices with their start and end apart: 3, of which 3 were waited for; matrix products, arithmetic and copies ran while one was open for 0% of the time, Pallas kernels for 0%

commit v1 on v0

--- a/solution.py
+++ b/solution.py
@@ -58,7 +58,12 @@
     local_params = inner_params[0, 0]
     summed = owned_sum(local_params)
     outer_next, moment_next = nesterov(outer_params[0], outer_momentum[0], summed, replicas)
-    synced = lax.all_gather(outer_next.astype(jnp.bfloat16), "replica", axis=0, tiled=True)
+    synced = jnp.concatenate(
+        lax.all_to_all(
+            jnp.stack([outer_next.astype(jnp.bfloat16)] * lax.axis_size("replica")), "replica", 0, 0
+        ),
+        axis=0,
+    )
     return (outer_next[None], moment_next[None], synced[None])
 
 

time: 876 us -> 781 us (0.89)
  the two profiles are of different devices: /device:TPU:1 before, /device:TPU:33 now
where the time goes in v1:
time: 781 us; the launch traced here: 780 us
  waiting for transfers between devices  732 us (94%)
  starting transfers between devices  17.3 us (2%)
  between operations  15.6 us (2%)
    reduce_scatter x1, waiting for transfers between devices, owned_sum(): lax.psum_scatter(local_params.astype(jnp.float32), 'replica', scatter_dim...  673 us
    all_to_all x1, waiting for transfers between devices, sync_fragment(): lax.all_to_all(jnp.stack([outer_next.astype(jnp.bfloat16)] * lax.axis_siz...  58.8 us
    all_to_all x1, starting transfers between devices, sync_fragment(): lax.all_to_all(jnp.stack([outer_next.astype(jnp.bfloat16)] * lax.axis_siz...  17.2 us
  transfers between devices with their start and end apart: 3, of which 2 were waited for; matrix products, arithmetic and copies ran while one was open for 1% of the time, Pallas kernels for 0%

profile of v1, /device:TPU:33, one launch (start us, length us, event | category | flops | bytes accessed | tf_op | source)
XLA Modules:
  0.0 780.3 jit_solution(4626228207602336604)
XLA Ops:
  8.0 0.0 copy-start
  8.0 0.0 copy-start.4
  8.0 0.0 copy-start.1
  8.0 0.0 reduce-scatter.2.cloned.1.call-start
  8.1 3.0 bitcast_convert_fusion
  11.1 0.0 reduce-scatter.2.cloned.1.call-update
  11.1 0.0 all-gather.2.cloned.1.call-start
  11.2 0.0 copy-done.4
  11.2 0.0 copy-done.1
  11.2 0.0 copy-start.2
  11.2 0.0 copy-start.3
  11.2 0.3 fusion
  11.6 1.3 fusion.2
  12.8 0.0 all-gather.2.cloned.1.call-update
  12.9 672.8 %reduce-scatter.2.cloned.1.call-done = f32[16,512]{1,0:T(8,128)} async-done(((f32[1024,512]{1,0:T(8,128)}), f32[16,512]{1,0:T(8,128)}) %reduce-scatter.2.cloned.1.call-update) | async-done | bytes 32784 | tf_op jit(solution)/shard_map/reduce_scatter | solution.py:51
  685.6 0.0 copy-done.2
  685.6 0.0 copy-done.3
  685.6 1.4 fusion.17
  687.0 1.2 stack.2
  688.2 17.2 %all-to-all-start = ((bf16[64,16,512]{2,1,0:T(8,128)(2,1)}), bf16[64,16,512]{2,1,0:T(8,128)(2,1)S(1)}, u32[]{:S(2)}, u32[]{:S(2)}) async-start(bf16[64,16,512]{2,1,0:T(8,128)(2,1)} %stack.2), calls=%async_computation.1 | async-start | bytes 2097152 | tf_op jit(solution)/shard_map/all_to_all | solution.py:62
  705.5 58.8 %all-to-all-done = bf16[64,16,512]{2,1,0:T(8,128)(2,1)S(1)} async-done(((bf16[64,16,512]{2,1,0:T(8,128)(2,1)}), bf16[64,16,512]{2,1,0:T(8,128)(2,1)S(1)}, u32[]{:S(2)}, u32[]{:S(2)}) %all-to-all-start) | async-done | bytes 1048608 | tf_op jit(solution)/shard_map/all_to_all | solution.py:62
  764.2 0.0 all-gather.2.cloned.1.call-done
  764.2 0.0 copy-done
  764.2 6.3 fusion.5
  770.5 0.6 fusion.13
  771.1 0.8 copy.10
  771.9 1.0 copy.12
  (5 shorter events, 0.0 us)
Async XLA Ops:
  8.0 756.2 %copy-start = (bf16[1,8192,128]{2,1,0:T(8,128)(2,1)S(1)}, bf16[1,8192,128]{2,1,0:T(8,128)(2,1)}, u32[]{:S(2)}) copy-start(bf16[1,8192,128]{2,1,0:T(8,128)(2,1)} %param.8) | copy-start | bytes 6291460
  8.0 3.2 copy-start.4
  8.0 3.2 copy-start.1
  8.0 677.6 %reduce-scatter.2.cloned.1.call-start = ((), (), s32[]{:S(2)}) async-start(), calls=%async_computation.3 | async-start | bytes 2129920 | tf_op jit(solution)/shard_map/reduce_scatter | solution.py:51
  11.1 753.1 %all-gather.2.cloned.1.call-start = ((), (), s32[]{:S(2)}) async-start(), calls=%async_computation.2 | async-start | bytes 9437184 | tf_op jit(solution)/shard_map/all_gather | solution.py:37
  11.2 674.4 %copy-start.2 = (f32[1,16,512]{2,1,0:T(8,128)S(1)}, f32[1,16,512]{2,1,0:T(8,128)}, u32[]{:S(2)}) copy-start(f32[1,16,512]{2,1,0:T(8,128)} %param.11) | copy-start | bytes 98308
  11.2 674.4 %copy-start.3 = (f32[1,16,512]{2,1,0:T(8,128)S(1)}, f32[1,16,512]{2,1,0:T(8,128)}, u32[]{:S(2)}) copy-start(f32[1,16,512]{2,1,0:T(8,128)} %param.10) | copy-start | bytes 98308
  688.2 76.0 %all-to-all-start = ((bf16[64,16,512]{2,1,0:T(8,128)(2,1)}), bf16[64,16,512]{2,1,0:T(8,128)(2,1)S(1)}, u32[]{:S(2)}, u32[]{:S(2)}) async-start(bf16[64,16,512]{2,1,0:T(8,128)(2,1)} %stack.2), calls=%async_computation.1 | async-start | bytes 2097152 | tf_op jit(solution)/shard_map/all_to_all | solution.py:62
Sparse Core Ops, SparseCore 0:
  11.7 673.9 reduce-scatter.1
Sparse Core Ops, SparseCore 1:
  14.3 180.6 all-gather.1
